TPU v7x, 512 devices: a whole 4x4x16 slice. The times are simulated.
512 devices in a mesh: dp: 128 (over y_lo, z, x), fsdp: 4 (over y_hi, core).
Axes of the slice: x: 4, y: 4 (y_hi: 2, y_lo: 2; y = y_hi * 2 + y_lo), z: 16, core: 2. Of those that a mesh axis runs over, the one named last changes fastest.
Arguments:
- cached: bfloat16 [128, 4, 256, 1024], P('dp', 'fsdp'), may hold values from -60 to 60
- send_rows: int32 [128, 4, 128, 4], P('dp', 'fsdp'), may hold values from -1 to 255, as said below
- take_rows: int32 [128, 4, 256], P('dp', 'fsdp'), may hold values from -1 to 511, as said below
- utt_index: int32 [128, 4, 256], P('dp', 'fsdp'), may hold values from 0 to 9, never falling along the last dimension, each value on 1 to 64 neighbouring positions
- upstream: bfloat16 [128, 4, 512, 1536], P('dp', 'fsdp'), may hold values from -6 to 6
- in_proj: bfloat16 [512, 1536], P(None, 'fsdp'), may hold values from -2 to 2
- norm_gain: bfloat16 [1536], P('fsdp'), may hold values from 0.099609375 to 1.8984375
- conv_kernel: bfloat16 [31, 1536], P(None, 'fsdp'), may hold values from -1 to 1
Outputs:
- grad_proj: float32 [512, 1536], P(None, 'fsdp')
- grad_kernel: float32 [31, 1536], P(None, 'fsdp')
- grad_gain: float32 [1536], P('fsdp')
- step_loss: float32 [128, 4], P('dp', 'fsdp')
Inputs may be any that keep to these rules, and one draw needn't show every extreme that they name: `send_rows`: entry [s, g, d, j] is -1 or the cache row of sender s (same fsdp group g) sent as entry j of its slot for device d. The used entries of a slot come first; a sender's used entries for one device lie in one aligned block of 4 cache rows; a sender's entries name distinct rows. Each device receives from 64 senders of its group, and some device of each group receives 4 rows from each of them. `take_rows`: entry [d, g, r] is -1 or s * 4 + j for a used entry send_rows[s, g, d, j]; each used entry is named once. The -1 entries of a device come last, the rows from one sender stand together, and some device of each group has no -1 entry. Sender 128 - 1 fills its whole slot for every device that it serves.
All inputs are finite; a program needn't handle non-finite values.
Results may differ from a plain program's by a relative error of at most 0.003.
Values may be sent and summed in bfloat16 or wider, within the bound.
A program may use at most 64 MiB of HBM per device.

v0:
```python
import jax
import jax.numpy as jnp
from jax import lax
from jax.sharding import PartitionSpec as P


def spread_conv(source_field, kernel_taps, tap_weights):
    tap_count = kernel_taps.shape[0]
    half_width = tap_count // 2
    step_count = source_field.shape[0]
    padded = jnp.pad(source_field, ((half_width, half_width), (0, 0)))
    summed = jnp.zeros_like(source_field)
    for offset in range(tap_count):
        summed = summed + kernel_taps[offset] * (
            tap_weights[:, offset : offset + 1] * padded[offset : offset + step_count]
        )
    return summed


def build_mask(live_steps, utterances, tap_count):
    half_width = tap_count // 2
    step_count = live_steps.shape[0]
    live_pad = jnp.pad(live_steps, (half_width, half_width))
    utter_pad = jnp.pad(utterances, (half_width, half_width), constant_values=-1)
    columns = []
    for offset in range(tap_count):
        columns.append(
            live_steps
            & live_pad[offset : offset + step_count]
            & (utterances == utter_pad[offset : offset + step_count])
        )
    return jnp.stack(columns, axis=1).astype(jnp.float32)


def layer_terms(encoded, live_steps, utterances, grad_above, gain, kernel):
    tap_count = kernel.shape[0]
    half_width = tap_count // 2
    step_count = encoded.shape[0]
    tap_weights = build_mask(live_steps, utterances, tap_count)
    row_mean = jnp.mean(encoded, axis=1, keepdims=True)
    centered = encoded - row_mean
    row_var = jnp.mean(centered * centered, axis=1, keepdims=True)
    inv_std = lax.rsqrt(row_var + 1e-05)
    normalized = centered * inv_std
    gain_f32 = gain.astype(jnp.float32)
    kernel_taps = kernel.astype(jnp.float32)
    normed = normalized * gain_f32
    conv_out = spread_conv(normed, kernel_taps, tap_weights)
    gate_sig = jax.nn.sigmoid(conv_out)
    output = encoded + conv_out * gate_sig
    scale = (encoded.shape[0] * encoded.shape[1]) ** (-0.5)
    grad_out = (
        jnp.where(live_steps[:, None], grad_above.astype(jnp.float32), jnp.zeros((), jnp.float32))
        * scale
    )
    device_loss = jnp.sum(output * grad_out)
    grad_conv = grad_out * (gate_sig * (1.0 + conv_out * (1.0 - gate_sig)))
    grad_normed = spread_conv(grad_conv, kernel_taps[::-1], tap_weights)
    padded = jnp.pad(normed, ((half_width, half_width), (0, 0)))
    grad_taps = jnp.stack(
        [
            jnp.sum(
                grad_conv
                * tap_weights[:, offset : offset + 1]
                * padded[offset : offset + step_count],
                axis=0,
            )
            for offset in range(tap_count)
        ]
    )
    grad_scale = jnp.sum(grad_normed * normalized, axis=0)
    grad_hat = grad_normed * gain_f32
    grad_x = grad_out + inv_std * (
        grad_hat
        - jnp.mean(grad_hat, axis=1, keepdims=True)
        - normalized * jnp.mean(grad_hat * normalized, axis=1, keepdims=True)
    )
    return (device_loss, grad_x.astype(jnp.bfloat16), grad_taps, grad_scale)


def per_device(cached, send_rows, take_rows, utt_index, upstream, in_proj, norm_gain, conv_kernel):
    cache_rows = cached[0, 0]
    wanted = send_rows[0, 0]
    outgoing = jnp.where(
        (wanted >= 0)[:, :, None],
        cache_rows[jnp.maximum(wanted, 0)],
        jnp.zeros((), cache_rows.dtype),
    )
    proj_full, taps_full, gain_full = (
        lax.all_gather(in_proj, "fsdp", axis=1, tiled=True),
        lax.all_gather(conv_kernel, "fsdp", axis=1, tiled=True),
        lax.all_gather(norm_gain[None, :], "fsdp", axis=1, tiled=True),
    )
    take_list = take_rows[0, 0]
    is_live = take_list >= 0
    safe_index = jnp.maximum(take_list, 0)
    pair_count = take_list.shape[0]
    step_width = cache_rows.shape[1] // 2
    arrived = lax.all_to_all(outgoing, "dp", split_axis=0, concat_axis=0, tiled=True)
    flat_rows = arrived.reshape(-1, arrived.shape[2])
    work_rows = jnp.where(is_live[:, None], flat_rows[safe_index], jnp.zeros((), flat_rows.dtype))
    frames = work_rows.reshape(2 * pair_count, step_width)
    encoded = jnp.dot(frames, proj_full, preferred_element_type=jnp.float32)
    live_steps = jnp.repeat(is_live, 2)
    utterances = jnp.repeat(utt_index[0, 0], 2)
    device_loss, grad_x, grad_taps, grad_scale = layer_terms(
        encoded, live_steps, utterances, upstream[0, 0], gain_full[0], taps_full
    )
    grad_weight = lax.dot_general(
        frames, grad_x, (((0,), (0,)), ((), ())), preferred_element_type=jnp.float32
    )
    shard_cols = in_proj.shape[1]
    totals = lax.psum((grad_weight, grad_taps, grad_scale[None, :]), ("dp", "fsdp"))
    col_start = lax.axis_index("fsdp") * shard_cols
    weight_part, taps_part, scale_part = [
        lax.dynamic_slice_in_dim(summed_item, col_start, shard_cols, 1) for summed_item in totals
    ]
    return (weight_part, taps_part, scale_part[0], device_loss.reshape(1, 1))


def solution(mesh):
    placed = (
        P("dp", "fsdp", None, None),
        P("dp", "fsdp", None, None),
        P("dp", "fsdp", None),
        P("dp", "fsdp", None),
        P("dp", "fsdp", None, None),
        P(None, "fsdp"),
        P("fsdp"),
        P(None, "fsdp"),
    )
    return jax.shard_map(
        per_device,
        mesh=mesh,
        in_specs=placed,
        out_specs=(P(None, "fsdp"), P(None, "fsdp"), P("fsdp"), P("dp", "fsdp")),
        check_vma=False,
    )
```

profile of v0, /device:TPU:2, one launch (start us, length us, event | category | flops | bytes accessed | tf_op | source)
XLA Modules:
  0.0 669.0 jit_solution(1528004560381405543)
XLA Ops:
  7.2 0.7 broadcast_maximum_fusion
  7.9 0.7 compare_bitcast_fusion
  8.9 2.1 gather_fusion
  10.9 0.4 reshape.99
  11.5 1.5 broadcast_select_fusion
  13.1 20.4 %all-to-all-start = ((bf16[128,4,1024]{2,1,0:T(4,128)(2,1)}), bf16[128,4,1024]{2,1,0:T(4,128)(2,1)S(1)}, u32[]{:S(2)}, u32[]{:S(2)}) async-start(bf16[128,4,1024]{2,1,0:T(4,128)(2,1)} %broadcast_select_fusion), calls=%async_computation | async-start | bytes 2097152 | tf_op jit(solution)/shard_map/all_to_all | solution.py:99
  33.6 0.7 all-gather.4.cloned.1.call-update
  35.9 0.2 stack.220
  36.1 6.7 all-gather.1
  42.8 6.9 %all_gather.10 = bf16[31,1536]{1,0:T(8,128)(2,1)S(1)} all-gather(bf16[31,384]{1,0:T(8,128)(2,1)S(1)} %copy-done.2), channel_id=1, replica_groups=mesh['dp'=128,'fsdp'=4] {'fsdp'}, dimensions={1}, use_global_device_ids=true | all-gather | bytes 119040 | tf_op jit(solution)/shard_map/all_gather | solution.py:91
  49.7 0.2 slice_reduce_fusion.29
  49.9 0.3 slice_reduce_fusion.30
  50.3 35.1 %all-to-all-done = bf16[128,4,1024]{2,1,0:T(4,128)(2,1)S(1)} async-done(((bf16[128,4,1024]{2,1,0:T(4,128)(2,1)}), bf16[128,4,1024]{2,1,0:T(4,128)(2,1)S(1)}, u32[]{:S(2)}, u32[]{:S(2)}) %all-to-all-start) | async-done | bytes 1048608 | tf_op jit(solution)/shard_map/all_to_all | solution.py:99
  85.5 0.3 reshape.93
  85.7 1.2 gather_fusion.1
  86.9 0.2 gather.10
  87.1 2.5 fusion.109
  89.6 0.5 multiply_reduce_fusion.33
  90.1 0.5 fusion.8
  90.6 0.9 copy-done.1
  91.5 31.9 %multiply_reduce_fusion.1 = (f32[1536]{0:T(1024)S(1)}, f32[1536]{0:T(1024)S(1)}, f32[1536]{0:T(1024)S(1)}, f32[1536]{0:T(1024)S(1)}, f32[1536]{0:T(1024)S(1)}, /...) fusion(f32[512,1536]{1,0:T(8,128)S(1)} %fusion.8, ...), kind=kLoop, calls=%fused_computation.10 | loop fusion | flops 102222336 | bytes 11319808 | tf_op jit(solution)/shard_map/reduce_sum | solution.py:62
  123.4 6.8 %multiply_reduce_fusion.10 = (f32[1536]{0:T(1024)S(1)}, f32[1536]{0:T(1024)S(1)}, f32[1536]{0:T(1024)S(1)}, f32[1536]{0:T(1024)S(1)}, f32[1536]{0:T(1024)S(1)}, ...) fusion(f32[512,1536]{1,0:T(8,128)S(1)} %get-tuple-element.72, ...), kind=kLoop, calls=%fused_computation.19 | loop fusion | flops 21219840 | bytes 6365184 | tf_op jit(solution)/shard_map/reduce_sum | solution.py:62
  130.2 6.6 multiply_reduce_fusion.16
  136.8 3.1 multiply_reduce_fusion.20
  140.3 28.3 %multiply_reduce_fusion = (f32[1536]{0:T(1024)S(1)}, f32[512]{0:T(512)S(1)}, f32[512]{0:T(512)S(1)}, f32[]{:T(128)}, f32[512,1536]{1,0:T(8,128)S(1)}) fusion(f32[512,1536]{1,0:T(8,128)S(1)} %get-tuple-element.137, f32[512]{0:T(512)S(1)} %add_rsqrt_fusion, f32[512]{0:T(512)S(1)} %broadcast_multiply_fusion.2, f32[1536]{0:T(1024)S(1)} %reshape.122, ...), kind=kLoop, calls=%fused_computation.9 | loop fusion | flops 86504960 | bytes 14430724 | tf_op jit(solution)/shard_map/reduce_sum | solution.py:71
  168.6 3.6 fusion.9
  172.1 2.8 stack.252
  174.9 104.0 %psum.23 = f32[1,1536]{1,0:T(1,128)S(1)} all-reduce(f32[1,1536]{1,0:T(1,128)S(1)} %broadcast_in_dim.73), channel_id=1, replica_groups=mesh['dp'=128,'fsdp'=4] {'dp','fsdp'}, use_global_device_ids=true, to_apply=%region_38.39 | all-reduce | flops 1536 | bytes 12288 | tf_op jit(solution)/shard_map/psum | solution.py:113
  279.0 0.6 dynamic-slice_reduce_fusion
  279.6 379.1 %all-reduce.7.cloned.1.call-done = (f32[512,1536]{1,0:T(8,128)}, f32[31,1536]{1,0:T(8,128)}) async-done(((f32[512,1536]{1,0:T(8,128)}, f32[31,1536]{1,0:T(8,128)}), (f32[512,1536]{1,0:T(8,128)}, f32[31,1536]{1,0:T(8,128)})) %all-reduce.7.cloned.1.call-update) | async-done | bytes 3336208 | tf_op jit(solution)/shard_map/psum | solution.py:113
  658.7 2.1 constant_dynamic-slice_fusion.1
  660.8 1.4 constant_dynamic-slice_fusion
  (105 shorter events, 2.2 us)
Async XLA Ops:
  7.2 1.7 copy-start
  10.9 23.4 %copy-start.5 = (s32[1,1,256]{2,1,0:T(1,128)S(1)}, s32[1,1,256]{2,1,0:T(1,128)}, u32[]{:S(2)}) copy-start(s32[1,1,256]{2,1,0:T(1,128)} %param.10) | copy-start | bytes 3076
  10.9 23.7 %copy-start.3 = (s32[1,1,256]{2,1,0:T(1,128)S(1)}, s32[1,1,256]{2,1,0:T(1,128)}, u32[]{:S(2)}) copy-start(s32[1,1,256]{2,1,0:T(1,128)} %param.11) | copy-start | bytes 3076
  11.4 24.7 %copy-start.4 = (bf16[384]{0:T(512)(128)(2,1)S(1)}, bf16[384]{0:T(512)(128)(2,1)}, u32[]{:S(2)}) copy-start(bf16[384]{0:T(512)(128)(2,1)} %param.14) | copy-start | bytes 2308
  11.4 31.4 %copy-start.2 = (bf16[31,384]{1,0:T(8,128)(2,1)S(1)}, bf16[31,384]{1,0:T(8,128)(2,1)}, u32[]{:S(2)}) copy-start(bf16[31,384]{1,0:T(8,128)(2,1)} %param.15) | copy-start | bytes 71428
  13.1 72.4 %all-to-all-start = ((bf16[128,4,1024]{2,1,0:T(4,128)(2,1)}), bf16[128,4,1024]{2,1,0:T(4,128)(2,1)S(1)}, u32[]{:S(2)}, u32[]{:S(2)}) async-start(bf16[128,4,1024]{2,1,0:T(4,128)(2,1)} %broadcast_select_fusion), calls=%async_computation | async-start | bytes 2097152 | tf_op jit(solution)/shard_map/all_to_all | solution.py:99
  33.5 53.6 %all-gather.4.cloned.1.call-start = ((), (), s32[]{:S(2)}) async-start(), calls=%async_computation.1 | async-start | bytes 1966080 | tf_op jit(solution)/shard_map/all_gather | solution.py:90
  34.2 624.5 %all-reduce.7.cloned.1.call-start = ((), (), s32[]{:S(2)}) async-start(), calls=%async_computation.2 | async-start | bytes 6684672 | tf_op jit(solution)/shard_map/psum | solution.py:113
  90.1 1.4 copy-start.1
Sparse Core Ops, SparseCore 0:
  36.5 35.0 all-gather.3
  175.0 483.6 all-reduce.6
where the time goes:
time: 669 us
  waiting for transfers between devices  415 us (62%)
  blocking collectives  118 us (18%)
  other arithmetic  80.9 us (12%)
  starting transfers between devices  20.5 us (3%)
  between operations  14.8 us (2%)
  local copies, waits for them, and re-layouts  14.2 us (2%)
    psum x1, waiting for transfers between devices, per_device(): lax.psum((grad_weight, grad_taps, grad_scale[None, :]), ('dp', 'fsdp'))  379 us
    psum x1, blocking collectives, per_device(): lax.psum((grad_weight, grad_taps, grad_scale[None, :]), ('dp', 'fsdp'))  104 us
    reduce_sum x4, other arithmetic, layer_terms(): jnp.sum(grad_conv * tap_weights[:, offset:offset + 1] * padded[offset:off...  48.3 us
    all_to_all x1, waiting for transfers between devices, per_device(): lax.all_to_all(outgoing, 'dp', split_axis=0, concat_axis=0, tiled=True)  35.1 us
    reduce_sum x1, other arithmetic, layer_terms(): grad_scale = jnp.sum(grad_normed * normalized, axis=0)  28.3 us
    all_to_all x1, starting transfers between devices, per_device(): lax.all_to_all(outgoing, 'dp', split_axis=0, concat_axis=0, tiled=True)  20.4 us
  transfers between devices with their start and end apart: 3, of which 2 were waited for; matrix products, arithmetic and copies ran while one was open for 1% of the time, Pallas kernels for 0%

commit v1 on v0

--- a/solution.py
+++ b/solution.py
@@ -110,7 +110,7 @@
         frames, grad_x, (((0,), (0,)), ((), ())), preferred_element_type=jnp.float32
     )
     shard_cols = in_proj.shape[1]
-    totals = lax.psum((grad_weight, grad_taps, grad_scale[None, :]), ("dp", "fsdp"))
+    totals = lax.psum(lax.psum((grad_weight, grad_taps, grad_scale[None, :]), "dp"), "fsdp")
     col_start = lax.axis_index("fsdp") * shard_cols
     weight_part, taps_part, scale_part = [
         lax.dynamic_slice_in_dim(summed_item, col_start, shard_cols, 1) for summed_item in totals

time: 669 us -> 1670 us (2.50)
  the two profiles are of different devices: /device:TPU:2 before, /device:TPU:24 now
where the time goes in v1:
time: 1670 us
  waiting for transfers between devices  1200 us (72%)
  blocking collectives  331 us (20%)
  other arithmetic  80.9 us (5%)
  starting transfers between devices  20.8 us (1%)
    psum x1, waiting for transfers between devices, per_device(): lax.psum((grad_weight, grad_taps, grad_scale[None, :]), 'dp')  1160 us
    psum x1, blocking collectives, per_device(): lax.psum((grad_weight, grad_taps, grad_scale[None, :]), 'dp')  310 us
    reduce_sum x4, other arithmetic, layer_terms(): jnp.sum(grad_conv * tap_weights[:, offset:offset + 1] * padded[offset:off...  48.3 us
    all_to_all x1, waiting for transfers between devices, per_device(): lax.all_to_all(outgoing, 'dp', split_axis=0, concat_axis=0, tiled=True)  39.4 us
  transfers between devices with their start and end apart: 4, of which 2 were waited for; matrix products, arithmetic and copies ran while one was open for 0% of the time, Pallas kernels for 0%

profile of v1, /device:TPU:24, one launch (start us, length us, event | category | flops | bytes accessed | tf_op | source)
XLA Modules:
  0.0 1669.2 jit_solution(9673941785845726212)
XLA Ops:
  7.2 0.7 broadcast_maximum_fusion
  7.9 0.7 compare_bitcast_fusion
  8.9 2.1 gather_fusion
  10.9 0.4 reshape.99
  11.5 1.5 broadcast_select_fusion
  13.1 20.7 %all-to-all-start = ((bf16[128,4,1024]{2,1,0:T(4,128)(2,1)}), bf16[128,4,1024]{2,1,0:T(4,128)(2,1)S(1)}, u32[]{:S(2)}, u32[]{:S(2)}) async-start(bf16[128,4,1024]{2,1,0:T(4,128)(2,1)} %broadcast_select_fusion), calls=%async_computation | async-start | bytes 2097152 | tf_op jit(solution)/shard_map/all_to_all | solution.py:99
  33.8 0.7 all-gather.4.cloned.1.call-update
  36.1 0.2 stack.220
  36.3 6.7 all-gather.1
  43.0 6.9 all_gather.10
  50.0 0.2 slice_reduce_fusion.29
  50.2 0.3 slice_reduce_fusion.30
  50.5 39.4 %all-to-all-done = bf16[128,4,1024]{2,1,0:T(4,128)(2,1)S(1)} async-done(((bf16[128,4,1024]{2,1,0:T(4,128)(2,1)}), bf16[128,4,1024]{2,1,0:T(4,128)(2,1)S(1)}, u32[]{:S(2)}, u32[]{:S(2)}) %all-to-all-start) | async-done | bytes 1048608 | tf_op jit(solution)/shard_map/all_to_all | solution.py:99
  89.9 0.3 reshape.93
  90.2 1.2 gather_fusion.1
  91.6 2.5 fusion.109
  94.1 0.5 multiply_reduce_fusion.33
  94.6 0.5 fusion.8
  95.0 0.9 copy-done.1
  96.0 31.9 %multiply_reduce_fusion.1 = (f32[1536]{0:T(1024)S(1)}, f32[1536]{0:T(1024)S(1)}, f32[1536]{0:T(1024)S(1)}, f32[1536]{0:T(1024)S(1)}, f32[1536]{0:T(1024)S(1)}, /...) fusion(f32[512,1536]{1,0:T(8,128)S(1)} %fusion.8, ...), kind=kLoop, calls=%fused_computation.10 | loop fusion | flops 102222336 | bytes 11319808 | tf_op jit(solution)/shard_map/reduce_sum | solution.py:62
  127.9 6.8 multiply_reduce_fusion.10
  134.6 6.6 multiply_reduce_fusion.16
  141.3 3.1 multiply_reduce_fusion.20
  144.8 28.3 %multiply_reduce_fusion = (f32[1536]{0:T(1024)S(1)}, f32[512]{0:T(512)S(1)}, f32[512]{0:T(512)S(1)}, f32[]{:T(128)}, f32[512,1536]{1,0:T(8,128)S(1)}) fusion(f32[512,1536]{1,0:T(8,128)S(1)} %get-tuple-element.139, f32[512]{0:T(512)S(1)} %add_rsqrt_fusion, f32[512]{0:T(512)S(1)} %broadcast_multiply_fusion.2, f32[1536]{0:T(1024)S(1)} %reshape.122, ...), kind=kLoop, calls=%fused_computation.9 | loop fusion | flops 86504960 | bytes 14430724 | tf_op jit(solution)/shard_map/reduce_sum | solution.py:71
  173.0 3.6 fusion.9
  176.6 2.8 stack.252
  179.4 1161.7 %all-reduce.9.cloned.1.call-done = (f32[512,1536]{1,0:T(8,128)}, f32[31,1536]{1,0:T(8,128)}) async-done(((f32[512,1536]{1,0:T(8,128)}, f32[31,1536]{1,0:T(8,128)}), (f32[512,1536]{1,0:T(8,128)}, f32[31,1536]{1,0:T(8,128)})) %all-reduce.9.cloned.1.call-update) | async-done | bytes 3336208 | tf_op jit(solution)/shard_map/psum | solution.py:113
  1341.1 310.2 %psum.46 = f32[1,1536]{1,0:T(1,128)S(1)} all-reduce(f32[1,1536]{1,0:T(1,128)S(1)} %broadcast_in_dim.73), channel_id=1, replica_groups=mesh['dp'=128,'fsdp'=4] {'dp'}, use_global_device_ids=true, to_apply=%region_40.41 | all-reduce | flops 1536 | bytes 12288 | tf_op jit(solution)/shard_map/psum | solution.py:113
  1651.3 7.3 psum.47
  1658.6 0.6 dynamic-slice_reduce_fusion
  1659.2 2.1 constant_dynamic-slice_fusion.1
  1661.3 1.4 constant_dynamic-slice_fusion
  (109 shorter events, 2.4 us)
Async XLA Ops:
  7.2 1.7 copy-start
  10.9 23.6 %copy-start.5 = (s32[1,1,256]{2,1,0:T(1,128)S(1)}, s32[1,1,256]{2,1,0:T(1,128)}, u32[]{:S(2)}) copy-start(s32[1,1,256]{2,1,0:T(1,128)} %param.10) | copy-start | bytes 3076
  10.9 23.9 %copy-start.3 = (s32[1,1,256]{2,1,0:T(1,128)S(1)}, s32[1,1,256]{2,1,0:T(1,128)}, u32[]{:S(2)}) copy-start(s32[1,1,256]{2,1,0:T(1,128)} %param.11) | copy-start | bytes 3076
  11.4 24.9 %copy-start.4 = (bf16[384]{0:T(512)(128)(2,1)S(1)}, bf16[384]{0:T(512)(128)(2,1)}, u32[]{:S(2)}) copy-start(bf16[384]{0:T(512)(128)(2,1)} %param.14) | copy-start | bytes 2308
  11.4 31.6 %copy-start.2 = (bf16[31,384]{1,0:T(8,128)(2,1)S(1)}, bf16[31,384]{1,0:T(8,128)(2,1)}, u32[]{:S(2)}) copy-start(bf16[31,384]{1,0:T(8,128)(2,1)} %param.15) | copy-start | bytes 71428
  13.1 76.8 %all-to-all-start = ((bf16[128,4,1024]{2,1,0:T(4,128)(2,1)}), bf16[128,4,1024]{2,1,0:T(4,128)(2,1)S(1)}, u32[]{:S(2)}, u32[]{:S(2)}) async-start(bf16[128,4,1024]{2,1,0:T(4,128)(2,1)} %broadcast_select_fusion), calls=%async_computation | async-start | bytes 2097152 | tf_op jit(solution)/shard_map/all_to_all | solution.py:99
  33.7 57.8 %all-gather.4.cloned.1.call-start = ((), (), s32[]{:S(2)}) async-start(), calls=%async_computation.1 | async-start | bytes 1966080 | tf_op jit(solution)/shard_map/all_gather | solution.py:90
  34.5 1306.6 %all-reduce.9.cloned.1.call-start = ((), (), s32[]{:S(2)}) async-start(), calls=%async_computation.2 | async-start | bytes 6684672 | tf_op jit(solution)/shard_map/psum | solution.py:113
  94.6 1.4 copy-start.1
  179.4 1479.8 %all-reduce.11.cloned.1.call-start = ((), (), s32[]{:S(2)}) async-start(), calls=%async_computation.3 | async-start | bytes 6684672 | tf_op jit(solution)/shard_map/psum | solution.py:113
Sparse Core Ops, SparseCore 0:
  36.7 32.5 all-gather.3
  179.5 1161.5 all-reduce.8
  1344.4 83.6 all-reduce.10
